TPU v7x, 128 devices: a whole 4x4x4 slice. The times are simulated.
128 devices in a mesh: rep: 4 (over z), shard: 16 (over x, y_lo, core), tp: 2 (over y_hi).
Axes of the slice: x: 4, y: 4 (y_hi: 2, y_lo: 2; y = y_hi * 2 + y_lo), z: 4, core: 2. Of those that a mesh axis runs over, the one named last changes fastest.
Arguments:
- delta_inputs: bfloat16 [4, 2, 768, 2304], P('rep', None, 'shard', 'tp'), may hold values from -6 to 6
- delta_mixing: bfloat16 [4, 2, 768, 768], P('rep', None, 'shard', 'tp'), may hold values from -6 to 6
- delta_expand: bfloat16 [4, 2, 768, 3072], P('rep', None, 'shard', 'tp'), may hold values from -6 to 6
- delta_reduce: bfloat16 [4, 2, 3072, 768], P('rep', None, 'shard', 'tp'), may hold values from -6 to 6
- owner_weights: float32 [4, 16, 2, 110592], P('rep', 'shard', 'tp'), may hold values from -6 to 6
- owner_momentum: float32 [4, 16, 2, 110592], P('rep', 'shard', 'tp'), may hold values from -6 to 6
- delta_embed: bfloat16 [4, 50304, 768], P('rep', 'shard', 'tp'), may hold values from -6 to 6
- embed_owner: float32 [16, 4, 786, 768], P('shard', 'rep', None, 'tp'), may hold values from -6 to 6
- embed_momentum: float32 [16, 4, 786, 64], P('shard', 'rep'), may hold values from -6 to 6
- basis: float32 [768, 64], P('tp'), may hold values from -0.21875 to 0.21875
Outputs:
- fresh_inputs: bfloat16 [2, 768, 2304], P(None, 'shard', 'tp')
- fresh_mixing: bfloat16 [2, 768, 768], P(None, 'shard', 'tp')
- fresh_expand: bfloat16 [2, 768, 3072], P(None, 'shard', 'tp')
- fresh_reduce: bfloat16 [2, 3072, 768], P(None, 'shard', 'tp')
- next_weights: float32 [4, 16, 2, 110592], P('rep', 'shard', 'tp')
- next_momentum: float32 [4, 16, 2, 110592], P('rep', 'shard', 'tp')
- fresh_embed: bfloat16 [50304, 768], P('shard', 'tp')
- next_embed: float32 [16, 4, 786, 768], P('shard', 'rep', None, 'tp')
- next_embed_momentum: float32 [16, 4, 786, 64], P('shard', 'rep')
All inputs are finite; a program needn't handle non-finite values.
Results may differ from a plain program's by a relative error of at most 0.0085.
Values may be sent and summed in bfloat16 or wider, within the bound.
A program may use at most 64 MiB of HBM per device.

v0:
```python
import jax
import jax.numpy as jnp
from jax import lax
from jax.experimental import pallas as pl
from jax.experimental.pallas import tpu as pltpu
from jax.sharding import PartitionSpec as P

MOMENTUM = 0.5
OUTER_RATE = 0.7
MESH = pl.DeviceIdType.MESH
F32 = jnp.float32
BF16 = jnp.bfloat16

GROUPS = 4
PEERS = 16
ROWS = 786
VROWS = 3144
WIDTH = 384
RANK = 64
FLAT_ROWS = 864
PACK = 416
HALF = 208
STAGE = 800
CHUNK = 448

W_IN, W_MIX, W_EXP, W_RED = 72, 24, 96, 24


def lanes(rows):
    return lax.broadcasted_iota(jnp.int32, (rows, 128), 1)


def tile(x, index):
    return x[:, index * 128 : (index + 1) * 128]


def turn(x, shift):
    shift = shift % 128
    return x if shift == 0 else pltpu.roll(x, shift, 1)


def place(total, lane, x, low, high):
    if total is None:
        return x
    return jnp.where((lane >= low) & (lane < high), x, total)


def piece(total, lane, src, start, width, to):
    first, last = start // 128, (start + width - 1) // 128
    shift = to - start % 128
    cut = width if first == last else last * 128 - start
    total = place(total, lane, turn(tile(src, first), shift), to, to + cut)
    if first != last:
        total = place(total, lane, turn(tile(src, last), shift), to + cut, to + width)
    return total


def split_columns(kinds, send_ref):
    inputs, mixing, expand, reduces = kinds
    lane = lanes(24)
    for u in range(PEERS):
        a = piece(None, lane, inputs, u * W_IN, W_IN, 0)
        a = piece(a, lane, mixing, u * W_MIX, W_MIX, W_IN)
        b = piece(None, lane, expand, u * W_EXP, W_EXP, 0)
        c = None
        for j in range(4):
            c = piece(c, lane, reduces[j], u * W_RED, W_RED, j * W_RED)
        send_ref[u] = jnp.concatenate([a, b, c], axis=1).astype(BF16)


def merge_columns(recv_ref):
    lane = lanes(24)
    blocks = [recv_ref[s].astype(F32) for s in range(PEERS)]

    def kind(which, width, base):
        out = []
        for t in range(PEERS * width // 128):
            total = None
            for s in range(PEERS):
                low, high = max(s * width - t * 128, 0), min((s + 1) * width - t * 128, 128)
                if low >= high:
                    continue
                shifted = turn(tile(blocks[s], which), s * width - t * 128 - base)
                total = place(total, lane, shifted, low, high)
            out.append(total)
        return out

    return (
        kind(0, W_IN, 0),
        kind(0, W_MIX, W_IN),
        kind(1, W_EXP, 0),
        [kind(2, W_RED, j * W_RED) for j in range(4)],
    )


def to_flat(kinds, flat_ref):
    inputs, mixing, expand, reduces = kinds
    for base, tiles in (
        [(0, inputs), (216, mixing), (288, expand)] + [(576 + 72 * j, reduces[j]) for j in range(4)]
    ):
        count = len(tiles)
        for t in range(count):
            flat_ref[pl.ds(base + t, 24, count), :] = tiles[t]


def from_flat(flat_ref):
    def rows(base, count):
        return jnp.concatenate(
            [flat_ref[pl.ds(base + t, 24, count), :] for t in range(count)], axis=1
        )

    return rows(0, 9), rows(216, 3), rows(288, 12), [rows(576 + 72 * j, 3) for j in range(4)]


def kinds_of(top, low):
    inputs, mixing = top[:24], top[24:, :384]
    expand = jnp.concatenate([low[:24], low[24:, :384]], axis=1)
    reduces = [top[24:, 384:768], top[24:, 768:], low[24:, 384:768], low[24:, 768:]]
    return inputs, mixing, expand, reduces


def halves_of(inputs, mixing, expand, reduces):
    top = jnp.concatenate(
        [inputs, jnp.concatenate([mixing, reduces[0], reduces[1]], axis=1)], axis=0
    )
    low = jnp.concatenate(
        [
            expand[:, :1152],
            jnp.concatenate([expand[:, 1152:], reduces[2], reduces[3]], axis=1),
        ],
        axis=0,
    )
    return top, low


def kernel(
    din_h, dmix_h, dexp_h, dred_h, w_h, m_h, de_h, eo_h, em_h, basis_h,
    fin_h, fmix_h, fexp_h, fred_h, wn_h, mn_h, fe_h, ne_h, nem_h,
    din, dmix, dexp, dred, w, m, de, eo, em, basis,
    fin, fmix, fexp, fred, wn, mn, fe, ne, nem,
    rs_send, rs_mid, rs_merge, rs_recv,
    a1_send, a1_recv, a2_send, a2_recv, flat, ag,
    coef, cf_send, cf_mid, cf_merge, cf_recv, tp_send, tp_recv, stage,
    in_sem, out_sem, z_send, z_recv, a1_ss, a1_rs, a2_ss, a2_rs, tp_ss, tp_rs,
):
    r, s, t = lax.axis_index("rep"), lax.axis_index("shard"), lax.axis_index("tp")
    right, left, opp = (r + 1) % GROUPS, (r + 3) % GROUPS, (r + 2) % GROUPS

    ins = [
        pltpu.make_async_copy(a, b, in_sem.at[i])
        for i, (a, b) in enumerate(
            [(din_h, din), (dmix_h, dmix), (dexp_h, dexp), (dred_h, dred), (basis_h, basis),
             (de_h, de), (em_h, em), (eo_h, eo), (w_h, w), (m_h, m)]
        )
    ]
    for c in ins:
        c.start()

    barrier = pltpu.get_barrier_semaphore()
    for z in (right, left):
        pl.semaphore_signal(barrier, inc=1, device_id={"rep": z}, device_id_type=MESH)
    for d in range(1, PEERS):
        pl.semaphore_signal(
            barrier, inc=1, device_id={"shard": (s + d) % PEERS}, device_id_type=MESH
        )
    pl.semaphore_signal(barrier, inc=1, device_id={"tp": 1 - t}, device_id_type=MESH)

    count = [0]

    def z_copy(src, dst, to):
        i = count[0]
        count[0] += 1
        return pltpu.make_async_remote_copy(
            src_ref=src, dst_ref=dst, send_sem=z_send.at[i], recv_sem=z_recv.at[i],
            device_id={"rep": to}, device_id_type=MESH,
        )

    for c in ins[:4]:
        c.wait()

    def pack(q, ref):
        return jnp.concatenate(
            [ref[l].astype(F32)[12 * q : 12 * q + 12] for l in range(2)], axis=0
        )

    for q in range(GROUPS):
        red = [dred[l, pl.ds(48 * q, 48), :].astype(F32) for l in range(2)]
        top, low = halves_of(
            pack(q, din), pack(q, dmix), pack(q, dexp),
            [red[0][:24], red[0][24:], red[1][:24], red[1][24:]],
        )
        rs_send[q, 0] = top.astype(BF16)
        rs_send[q, 1] = low.astype(BF16)

    pl.semaphore_wait(barrier, PEERS + 2)
    rs1 = [z_copy(rs_send.at[opp, 0], rs_mid.at[0], right),
           z_copy(rs_send.at[opp, 1], rs_mid.at[1], left)]
    for c in rs1:
        c.start()

    ins[4].wait()
    b = basis[...]
    b_hi = b.astype(BF16)
    b_lo = (b - b_hi.astype(F32)).astype(BF16)
    rhs = jnp.concatenate([b_hi, b_hi, b_lo, b_lo], axis=1)
    ins[5].wait()

    def terms(start, rows):
        y = jnp.dot(de[pl.ds(start, rows), :], rhs, preferred_element_type=F32)
        coef[pl.ds(start, rows), :] = y[:, :128] + y[:, 128:]

    def body(i, carry):
        terms(pl.multiple_of(i * CHUNK, CHUNK), CHUNK)
        return carry

    lax.fori_loop(0, VROWS // CHUNK, body, 0)
    terms(VROWS // CHUNK * CHUNK, VROWS % CHUNK)
    coef[pl.ds(VROWS, 56), :] = jnp.zeros((56, 128), F32)
    lane = lanes(PACK)
    for q in range(GROUPS):
        packed = jnp.where(
            lane < RANK, coef[pl.ds(ROWS * q, PACK), :], coef[pl.ds(ROWS * q + PACK, PACK), :]
        ).astype(BF16)
        cf_send[q, 0] = packed[:HALF]
        cf_send[q, 1] = packed[HALF:]
    cf1 = [z_copy(cf_send.at[opp, 0], cf_mid.at[0], right),
           z_copy(cf_send.at[opp, 1], cf_mid.at[1], left)]
    cf2 = [z_copy(cf_send.at[right, 1], cf_recv.at[1], right),
           z_copy(cf_send.at[left, 0], cf_recv.at[3], left)]
    rs2 = [z_copy(rs_send.at[right, 1], rs_recv.at[1], right),
           z_copy(rs_send.at[left, 0], rs_recv.at[3], left)]
    for c in cf1 + cf2 + rs2:
        c.start()

    for c in cf1:
        c.wait_recv()
    cf_merge[0] = (cf_send[right, 0].astype(F32) + cf_mid[0].astype(F32)).astype(BF16)
    cf_merge[1] = (cf_send[left, 1].astype(F32) + cf_mid[1].astype(F32)).astype(BF16)
    cf3 = [z_copy(cf_merge.at[0], cf_recv.at[0], right),
           z_copy(cf_merge.at[1], cf_recv.at[2], left)]
    for c in cf3:
        c.start()

    for c in rs1:
        c.wait_recv()
    rs_merge[0] = (rs_send[right, 0].astype(F32) + rs_mid[0].astype(F32)).astype(BF16)
    rs_merge[1] = (rs_send[left, 1].astype(F32) + rs_mid[1].astype(F32)).astype(BF16)
    rs3 = [z_copy(rs_merge.at[0], rs_recv.at[0], right),
           z_copy(rs_merge.at[1], rs_recv.at[2], left)]
    for c in rs3:
        c.start()

    for c in cf2 + cf3:
        c.wait_recv()

    def total(send, recv):
        top = send[r, 0].astype(F32) + (recv[0].astype(F32) + recv[3].astype(F32))
        low = send[r, 1].astype(F32) + (recv[1].astype(F32) + recv[2].astype(F32))
        return top, low

    top, low = total(cf_send, cf_recv)
    tp_send[pl.ds(0, HALF), :] = top.astype(BF16)
    tp_send[pl.ds(HALF, HALF), :] = low.astype(BF16)
    tp = pltpu.make_async_remote_copy(
        src_ref=tp_send, dst_ref=tp_recv, send_sem=tp_ss.at[0], recv_sem=tp_rs.at[0],
        device_id={"tp": 1 - t}, device_id_type=MESH,
    )
    tp.start()

    def exchange(send, recv, send_sem, recv_sem):
        copies = [
            pltpu.make_async_remote_copy(
                src_ref=send.at[(s + d) % PEERS], dst_ref=recv.at[s],
                send_sem=send_sem.at[d], recv_sem=recv_sem.at[d],
                device_id={"shard": (s + d) % PEERS}, device_id_type=MESH,
            )
            for d in range(1, PEERS)
        ]
        for c in copies:
            c.start()
        recv[s] = send[s]
        return copies

    for c in rs2 + rs3:
        c.wait_recv()
    top, low = total(rs_send, rs_recv)
    split_columns(kinds_of(top * 0.25, low * 0.25), a1_send)
    a1 = exchange(a1_send, a1_recv, a1_ss, a1_rs)

    for c in ins[6:8]:
        c.wait()
    tp.wait_recv()
    both = (tp_send[...].astype(F32) + tp_recv[...].astype(F32)) * 0.25
    dims = (((1,), (1,)), ((), ()))
    for start, rows, c in ((0, PACK, both), (PACK, ROWS - PACK, turn(both, RANK))):
        c = c[:rows, :RANK]
        momentum = MOMENTUM * em[pl.ds(start, rows), :] + c
        nem[pl.ds(start, rows), :] = momentum
        direction = c + MOMENTUM * momentum
        d_hi = direction.astype(BF16)
        d_lo = (direction - d_hi.astype(F32)).astype(BF16)
        update = lax.dot_general(d_hi, b_hi, dims, preferred_element_type=F32)
        update += lax.dot_general(d_lo, b_hi, dims, preferred_element_type=F32)
        update += lax.dot_general(d_hi, b_lo, dims, preferred_element_type=F32)
        table = eo[pl.ds(start, rows), :] - OUTER_RATE * update
        ne[pl.ds(start, rows), :] = table
        stage[r, pl.ds(start, rows), :] = table.astype(BF16)
    first, second = pl.ds(0, STAGE // 2), pl.ds(STAGE // 2, STAGE // 2)
    eg1 = [z_copy(stage.at[r, first], stage.at[r, first], right),
           z_copy(stage.at[r, second], stage.at[r, second], left)]
    eg2 = [z_copy(stage.at[r, second], stage.at[r, second], right),
           z_copy(stage.at[r, first], stage.at[r, first], left)]
    for c in eg1 + eg2:
        c.start()
    outs = [pltpu.make_async_copy(a, o, out_sem.at[i])
            for i, (a, o) in enumerate([(nem, nem_h), (ne, ne_h), (mn, mn_h), (wn, wn_h),
                                        (fin, fin_h), (fmix, fmix_h), (fexp, fexp_h),
                                        (fred, fred_h), (fe, fe_h)])]
    for c in outs[:2]:
        c.start()

    for c in ins[8:10]:
        c.wait()
    for c in a1:
        c.wait_recv()
    to_flat(merge_columns(a1_recv), flat)
    gradient = flat[...]
    momentum = MOMENTUM * m[...] + gradient
    mn[...] = momentum
    wn[...] = w[...] - OUTER_RATE * (gradient + MOMENTUM * momentum)
    split_columns(from_flat(wn), a2_send)
    a2 = exchange(a2_send, a2_recv, a2_ss, a2_rs)
    for c in outs[2:4]:
        c.start()

    for c in a2:
        c.wait_recv()
    inputs, mixing, expand, reduces = merge_columns(a2_recv)
    join = lambda tiles: jnp.concatenate(tiles, axis=1)
    top, low = halves_of(join(inputs), join(mixing), join(expand), [join(x) for x in reduces])
    ag[r, 0] = top.astype(BF16)
    ag[r, 1] = low.astype(BF16)
    dg1 = [z_copy(ag.at[r, 0], ag.at[r, 0], right), z_copy(ag.at[r, 1], ag.at[r, 1], left)]
    dg2 = [z_copy(ag.at[r, 1], ag.at[r, 1], right), z_copy(ag.at[r, 0], ag.at[r, 0], left)]
    for c in dg1 + dg2:
        c.start()

    for c in eg1:
        c.wait_recv()
    eg3 = [z_copy(stage.at[left, first], stage.at[left, first], right),
           z_copy(stage.at[right, second], stage.at[right, second], left)]
    for c in eg3:
        c.start()
    for c in dg1:
        c.wait_recv()
    dg3 = [z_copy(ag.at[left, 0], ag.at[left, 0], right),
           z_copy(ag.at[right, 1], ag.at[right, 1], left)]
    for c in dg3:
        c.start()

    for c in eg2 + eg3:
        c.wait_recv()
    for q in range(GROUPS):
        fe[pl.ds(ROWS * q, ROWS), :] = stage[q, pl.ds(0, ROWS), :]
    outs[8].start()

    for c in dg2 + dg3:
        c.wait_recv()
    parts = [kinds_of(ag[q, 0].astype(F32), ag[q, 1].astype(F32)) for q in range(GROUPS)]
    for l in range(2):
        for k, out in enumerate((fin, fmix, fexp)):
            out[l] = jnp.concatenate(
                [parts[q][k][12 * l : 12 * l + 12] for q in range(GROUPS)], axis=0
            ).astype(BF16)
        for q in range(GROUPS):
            fred[l, pl.ds(48 * q, 48), :] = jnp.concatenate(
                [parts[q][3][2 * l], parts[q][3][2 * l + 1]], axis=0
            ).astype(BF16)
    for c in outs[4:8]:
        c.start()

    for c in (rs1 + rs2 + rs3 + cf1 + cf2 + cf3 + [tp] + a1 + a2 + eg1 + eg2 + eg3
              + dg1 + dg2 + dg3):
        c.wait_send()
    for c in outs:
        c.wait()


def local(
    delta_inputs, delta_mixing, delta_expand, delta_reduce, owner_weights, owner_momentum,
    delta_embed, embed_owner, embed_momentum, basis,
):
    args = (
        delta_inputs[0], delta_mixing[0], delta_expand[0], delta_reduce[0],
        owner_weights.reshape(FLAT_ROWS, 128), owner_momentum.reshape(FLAT_ROWS, 128),
        delta_embed[0], embed_owner[0, 0], embed_momentum[0, 0], basis,
    )
    outs = (
        args[0], args[1], args[2], args[3], args[4], args[5], args[6], args[7], args[8],
    )
    vmem = lambda x: pltpu.VMEM(x.shape, x.dtype)
    dma = pltpu.SemaphoreType.DMA
    half = (48, 1152)
    results = pl.pallas_call(
        kernel,
        name="outer_step",
        out_shape=[jax.ShapeDtypeStruct(x.shape, x.dtype) for x in outs],
        in_specs=[pl.BlockSpec(memory_space=pl.ANY)] * 10,
        out_specs=[pl.BlockSpec(memory_space=pl.ANY)] * 9,
        scratch_shapes=[vmem(x) for x in args]
        + [vmem(x) for x in outs]
        + [
            pltpu.VMEM((GROUPS, 2) + half, BF16),
            pltpu.VMEM((2,) + half, BF16),
            pltpu.VMEM((2,) + half, BF16),
            pltpu.VMEM((4,) + half, BF16),
            pltpu.VMEM((PEERS, 24, 384), BF16),
            pltpu.VMEM((PEERS, 24, 384), BF16),
            pltpu.VMEM((PEERS, 24, 384), BF16),
            pltpu.VMEM((PEERS, 24, 384), BF16),
            pltpu.VMEM((FLAT_ROWS, 128), F32),
            pltpu.VMEM((GROUPS, 2) + half, BF16),
            pltpu.VMEM((VROWS + 56, 128), F32),
            pltpu.VMEM((GROUPS, 2, HALF, 128), BF16),
            pltpu.VMEM((2, HALF, 128), BF16),
            pltpu.VMEM((2, HALF, 128), BF16),
            pltpu.VMEM((4, HALF, 128), BF16),
            pltpu.VMEM((PACK, 128), BF16),
            pltpu.VMEM((PACK, 128), BF16),
            pltpu.VMEM((GROUPS, STAGE, WIDTH), BF16),
            dma((10,)),
            dma((9,)),
            dma((24,)),
            dma((24,)),
            dma((PEERS,)),
            dma((PEERS,)),
            dma((PEERS,)),
            dma((PEERS,)),
            dma((1,)),
            dma((1,)),
        ],
        compiler_params=pltpu.CompilerParams(
            collective_id=0, has_side_effects=True, vmem_limit_bytes=48 * 1024 * 1024
        ),
    )(*args)
    return (
        results[0], results[1], results[2], results[3],
        results[4].reshape(owner_weights.shape), results[5].reshape(owner_momentum.shape),
        results[6], results[7][None, None], results[8][None, None],
    )


def solution(mesh):
    in_specs = (
        P("rep", None, "shard", "tp"),
        P("rep", None, "shard", "tp"),
        P("rep", None, "shard", "tp"),
        P("rep", None, "shard", "tp"),
        P("rep", "shard", "tp", None),
        P("rep", "shard", "tp", None),
        P("rep", "shard", "tp"),
        P("shard", "rep", None, "tp"),
        P("shard", "rep", None, None),
        P("tp", None),
    )
    out_specs = (
        P(None, "shard", "tp"),
        P(None, "shard", "tp"),
        P(None, "shard", "tp"),
        P(None, "shard", "tp"),
        P("rep", "shard", "tp", None),
        P("rep", "shard", "tp", None),
        P("shard", "tp"),
        P("shard", "rep", None, "tp"),
        P("shard", "rep", None, None),
    )
    return jax.shard_map(local, mesh=mesh, in_specs=in_specs, out_specs=out_specs, check_vma=False)
```

profile of v0, /device:TPU:0, one launch (start us, length us, event | category | flops | bytes accessed | tf_op | source)
XLA Modules:
  0.0 70.1 jit_solution(4396952214574361604)
XLA Ops:
  0.6 1.0 %copy.20.basis_h = f32[384,64]{1,0:T(8,128)S(1)} copy(f32[384,64]{0,1:T(8,128)} %param.19) | data formatting | bytes 196608 | tf_op args[9]
  1.7 1.1 %copy.19 = f32[1,1,786,64]{3,2,1,0:T(8,128)S(1)} copy(f32[1,1,786,64]{2,3,1,0:T(8,128)} %param.18) | data formatting | bytes 402432 | tf_op args[8]
  2.8 0.0 copy-start
  2.8 0.0 copy-start.1
  2.8 0.0 copy-start.2
  2.8 0.0 copy-start.3
  2.8 0.0 copy-start.8
  2.8 0.0 copy-start.9
  2.9 2.5 %copy.25 = f32[1,1,786,384]{3,2,1,0:T(8,128)} copy(f32[1,1,786,384]{3,1,2,0:T(1,128)} %param.17) | data formatting | bytes 2414592
  5.4 0.0 copy-done
  5.4 0.0 copy-done.1
  5.4 0.0 copy-done.2
  5.4 0.0 copy-done.3
  5.4 0.0 copy-done.8
  5.4 0.0 copy-done.9
  5.4 54.4 %outer_step.1 = (bf16[2,48,1152]{2,1,0:T(8,128)(2,1)S(1)}, bf16[2,48,384]{2,1,0:T(8,128)(2,1)S(1)}, bf16[2,48,1536]{2,1,0:T(8,128)(2,1)S(1)}, bf16[2,192,384]{2,...) custom-call(bf16[2,48,1152]{2,1,0:T(8,128)(2,1)S(1)} %bitcast.24, ...), custom_call_target="tpu_custom_call" | custom-call | tf_op jit(solution)/shard_map/outer_step/pallas_call | solution.py:404
  59.8 0.0 copy-start.4
  59.8 0.7 %copy-done.4 = bf16[2,48,1536]{2,1,0:T(8,128)(2,1)} copy-done((bf16[2,48,1536]{2,1,0:T(8,128)(2,1)}, bf16[2,48,1536]{2,1,0:T(8,128)(2,1)S(1)}, u32[]{:S(2)}) %copy-start.4) | copy-done | bytes 294936
  60.5 0.0 copy-start.6
  60.5 0.7 copy-done.6
  61.2 0.9 %copy.22 = f32[1,1,786,64]{2,3,1,0:T(8,128)} copy(f32[1,1,786,64]{3,2,1,0:T(8,128)S(1)} %bitcast.21) | data formatting | bytes 402432
  62.1 0.0 copy-start.7
  62.1 0.0 copy-start.5
  62.1 2.3 %copy.21 = f32[1,1,786,384]{3,1,2,0:T(1,128)} copy(f32[1,1,786,384]{3,2,1,0:T(8,128)S(1)} %bitcast.16) | data formatting | bytes 2414592
  64.4 0.0 copy-done.7
  64.4 0.7 copy.33
  65.1 0.6 copy.34
  65.7 0.0 copy-done.5
  65.7 0.0 copy-start.10
  65.7 0.7 %copy.35 = bf16[2,48,1536]{2,1,0:T(8,128)(2,1)} copy(bf16[2,48,1536]{2,1,0:T(8,128)(2,1)S(1)} %copy-done.5) | data formatting | bytes 589824
  66.4 0.7 %copy.36 = bf16[2,192,384]{2,1,0:T(8,128)(2,1)} copy(bf16[2,192,384]{2,1,0:T(8,128)(2,1)S(1)} %get-tuple-element.48) | data formatting | bytes 589824
  67.1 0.8 %copy.37 = f32[1,1,1,110592]{3,2,1,0:T(1,128)} copy(f32[1,1,1,110592]{3,2,1,0:T(1,128)S(1)} %bitcast.20) | data formatting | bytes 884736
  67.9 0.8 %copy.38 = f32[1,1,1,110592]{3,2,1,0:T(1,128)} copy(f32[1,1,1,110592]{3,2,1,0:T(1,128)S(1)} %bitcast.19) | data formatting | bytes 884736
  68.7 0.0 copy-done.10
  68.7 1.4 %copy.39 = bf16[3144,384]{1,0:T(8,128)(2,1)} copy(bf16[3144,384]{1,0:T(8,128)(2,1)S(1)} %copy-done.10) | data formatting | bytes 4829184
Async XLA Ops:
  2.8 2.6 %copy-start = (f32[1,1,1,110592]{3,2,1,0:T(1,128)S(1)}, f32[1,1,1,110592]{3,2,1,0:T(1,128)}, u32[]{:S(2)}) copy-start(f32[1,1,1,110592]{3,2,1,0:T(1,128)} %param.14) | copy-start | bytes 1327108
  2.8 2.6 %copy-start.1 = (f32[1,1,1,110592]{3,2,1,0:T(1,128)S(1)}, f32[1,1,1,110592]{3,2,1,0:T(1,128)}, u32[]{:S(2)}) copy-start(f32[1,1,1,110592]{3,2,1,0:T(1,128)} %param.15) | copy-start | bytes 1327108
  2.8 2.6 %copy-start.2 = (bf16[1,2,48,1536]{3,2,1,0:T(8,128)(2,1)S(1)}, bf16[1,2,48,1536]{3,2,1,0:T(8,128)(2,1)}, u32[]{:S(2)}) copy-start(bf16[1,2,48,1536]{3,2,1,0:T(8,128)(2,1)} %param.12) | copy-start | bytes 884740
  2.8 2.6 %copy-start.3 = (bf16[1,2,192,384]{3,2,1,0:T(8,128)(2,1)S(1)}, bf16[1,2,192,384]{3,2,1,0:T(8,128)(2,1)}, u32[]{:S(2)}) copy-start(bf16[1,2,192,384]{3,2,1,0:T(8,128)(2,1)} %param.13) | copy-start | bytes 884740
  2.8 2.6 %copy-start.8 = (bf16[1,2,48,1152]{3,2,1,0:T(8,128)(2,1)S(1)}, bf16[1,2,48,1152]{3,2,1,0:T(8,128)(2,1)}, u32[]{:S(2)}) copy-start(bf16[1,2,48,1152]{3,2,1,0:T(8,128)(2,1)} %param.10) | copy-start | bytes 663556
  2.8 2.5 %copy-start.9 = (bf16[1,2,48,384]{3,2,1,0:T(8,128)(2,1)S(1)}, bf16[1,2,48,384]{3,2,1,0:T(8,128)(2,1)}, u32[]{:S(2)}) copy-start(bf16[1,2,48,384]{3,2,1,0:T(8,128)(2,1)} %param.11) | copy-start | bytes 221188
  59.8 0.7 %copy-start.4 = (bf16[2,48,1536]{2,1,0:T(8,128)(2,1)}, bf16[2,48,1536]{2,1,0:T(8,128)(2,1)S(1)}, u32[]{:S(2)}) copy-start(bf16[2,48,1536]{2,1,0:T(8,128)(2,1)S(1)} %get-tuple-element.47) | copy-start | bytes 884740
  60.5 0.7 copy-start.6
  62.1 2.3 %copy-start.7 = (bf16[2,48,1152]{2,1,0:T(8,128)(2,1)S(1)}, bf16[2,48,1152]{2,1,0:T(8,128)(2,1)}, u32[]{:S(2)}) copy-start(bf16[2,48,1152]{2,1,0:T(8,128)(2,1)} %copy-done.6) | copy-start | bytes 663556
  62.1 3.6 %copy-start.5 = (bf16[2,48,1536]{2,1,0:T(8,128)(2,1)S(1)}, bf16[2,48,1536]{2,1,0:T(8,128)(2,1)}, u32[]{:S(2)}) copy-start(bf16[2,48,1536]{2,1,0:T(8,128)(2,1)} %copy-done.4) | copy-start | bytes 884740
  65.7 3.0 %copy-start.10 = (bf16[3144,384]{1,0:T(8,128)(2,1)S(1)}, bf16[3144,384]{1,0:T(8,128)(2,1)}, u32[]{:S(2)}) copy-start(bf16[3144,384]{1,0:T(8,128)(2,1)} %get-tuple-element.51) | copy-start | bytes 7243780
where the time goes:
time: 70.3 us; the launch traced here: 70.1 us
  Pallas kernels  54.4 us (77%)
  local copies, waits for them, and re-layouts  14.9 us (21%)
  between operations  0.75 us (1%)
    pallas_call x1, Pallas kernels, local(): pl.pallas_call(kernel, name='outer_step', out_shape=[jax.ShapeDtypeStruct...  54.4 us
    unnamed x34, local copies, waits for them, and re-layouts  14.9 us

commit v1 on v0

--- a/solution.py
+++ b/solution.py
@@ -150,7 +150,7 @@
         pltpu.make_async_copy(a, b, in_sem.at[i])
         for i, (a, b) in enumerate(
             [(din_h, din), (dmix_h, dmix), (dexp_h, dexp), (dred_h, dred), (basis_h, basis),
-             (de_h, de), (em_h, em), (eo_h, eo), (w_h, w), (m_h, m)]
+             (de_h, de), (em_h, em), (eo_h.at[:, 0, :], eo), (w_h, w), (m_h, m)]
         )
     ]
     for c in ins:
@@ -202,11 +202,14 @@
     b = basis[...]
     b_hi = b.astype(BF16)
     b_lo = (b - b_hi.astype(F32)).astype(BF16)
-    rhs = jnp.concatenate([b_hi, b_hi, b_lo, b_lo], axis=1)
+    rhs = jnp.concatenate([b_hi, b_hi, b_lo, b_lo], axis=0)
+    across = (((1,), (1,)), ((), ()))
     ins[5].wait()
 
     def terms(start, rows):
-        y = jnp.dot(de[pl.ds(start, rows), :], rhs, preferred_element_type=F32)
+        y = lax.dot_general(
+            de[pl.ds(start, rows), :], rhs, across, preferred_element_type=F32
+        )
         coef[pl.ds(start, rows), :] = y[:, :128] + y[:, 128:]
 
     def body(i, carry):
@@ -291,20 +294,25 @@
         c.wait()
     tp.wait_recv()
     both = (tp_send[...].astype(F32) + tp_recv[...].astype(F32)) * 0.25
-    dims = (((1,), (1,)), ((), ()))
+    momenta = jnp.transpose(em[...])
+    kept = []
     for start, rows, c in ((0, PACK, both), (PACK, ROWS - PACK, turn(both, RANK))):
         c = c[:rows, :RANK]
-        momentum = MOMENTUM * em[pl.ds(start, rows), :] + c
-        nem[pl.ds(start, rows), :] = momentum
+        momentum = MOMENTUM * momenta[start : start + rows] + c
+        kept.append(momentum)
         direction = c + MOMENTUM * momentum
         d_hi = direction.astype(BF16)
         d_lo = (direction - d_hi.astype(F32)).astype(BF16)
-        update = lax.dot_general(d_hi, b_hi, dims, preferred_element_type=F32)
-        update += lax.dot_general(d_lo, b_hi, dims, preferred_element_type=F32)
-        update += lax.dot_general(d_hi, b_lo, dims, preferred_element_type=F32)
-        table = eo[pl.ds(start, rows), :] - OUTER_RATE * update
-        ne[pl.ds(start, rows), :] = table
-        stage[r, pl.ds(start, rows), :] = table.astype(BF16)
+        update = jnp.dot(d_hi, b_hi, preferred_element_type=F32)
+        update += jnp.dot(d_lo, b_hi, preferred_element_type=F32)
+        update += jnp.dot(d_hi, b_lo, preferred_element_type=F32)
+        parts = []
+        for j in range(WIDTH // 128):
+            place_of = pl.ds(3 * start + j, rows, 3)
+            table = eo[place_of, :] - OUTER_RATE * tile(update, j)
+            ne[place_of, :] = table
+            parts.append(table.astype(BF16))
+        stage[r, pl.ds(start, rows), :] = jnp.concatenate(parts, axis=1)
     first, second = pl.ds(0, STAGE // 2), pl.ds(STAGE // 2, STAGE // 2)
     eg1 = [z_copy(stage.at[r, first], stage.at[r, first], right),
            z_copy(stage.at[r, second], stage.at[r, second], left)]
@@ -312,6 +320,7 @@
            z_copy(stage.at[r, first], stage.at[r, first], left)]
     for c in eg1 + eg2:
         c.start()
+    nem[...] = jnp.transpose(jnp.concatenate(kept, axis=0))
     outs = [pltpu.make_async_copy(a, o, out_sem.at[i])
             for i, (a, o) in enumerate([(nem, nem_h), (ne, ne_h), (mn, mn_h), (wn, wn_h),
                                         (fin, fin_h), (fmix, fmix_h), (fexp, fexp_h),
@@ -386,6 +395,18 @@
         c.wait()
 
 
+def flush(*refs):
+    sem = refs[18]
+    copies = []
+    for i in range(9):
+        to = refs[9 + i].at[:, 0, :] if i == 7 else refs[9 + i]
+        copies.append(pltpu.make_async_copy(refs[i], to, sem.at[i]))
+    for c in copies:
+        c.start()
+    for c in copies:
+        c.wait()
+
+
 def local(
     delta_inputs, delta_mixing, delta_expand, delta_reduce, owner_weights, owner_momentum,
     delta_embed, embed_owner, embed_momentum, basis,
@@ -393,21 +414,23 @@
     args = (
         delta_inputs[0], delta_mixing[0], delta_expand[0], delta_reduce[0],
         owner_weights.reshape(FLAT_ROWS, 128), owner_momentum.reshape(FLAT_ROWS, 128),
-        delta_embed[0], embed_owner[0, 0], embed_momentum[0, 0], basis,
-    )
-    outs = (
-        args[0], args[1], args[2], args[3], args[4], args[5], args[6], args[7], args[8],
-    )
+        delta_embed[0],
+        jnp.transpose(embed_owner[0], (1, 0, 2)).reshape(3 * ROWS, 1, 128),
+        embed_momentum[0, 0].T, basis.T,
+    )
+    table = jax.ShapeDtypeStruct((3 * ROWS, 128), F32)
+    outs = args[:7] + (table, args[8])
     vmem = lambda x: pltpu.VMEM(x.shape, x.dtype)
     dma = pltpu.SemaphoreType.DMA
     half = (48, 1152)
+    args = tuple(pltpu.with_memory_space_constraint(x, pltpu.HBM) for x in args)
     results = pl.pallas_call(
         kernel,
         name="outer_step",
         out_shape=[jax.ShapeDtypeStruct(x.shape, x.dtype) for x in outs],
-        in_specs=[pl.BlockSpec(memory_space=pl.ANY)] * 10,
+        in_specs=[pl.BlockSpec(memory_space=pltpu.HBM)] * 10,
         out_specs=[pl.BlockSpec(memory_space=pl.ANY)] * 9,
-        scratch_shapes=[vmem(x) for x in args]
+        scratch_shapes=[vmem(x) for x in args[:7] + (table,) + args[8:]]
         + [vmem(x) for x in outs]
         + [
             pltpu.VMEM((GROUPS, 2) + half, BF16),
@@ -440,13 +463,24 @@
             dma((1,)),
         ],
         compiler_params=pltpu.CompilerParams(
-            collective_id=0, has_side_effects=True, vmem_limit_bytes=48 * 1024 * 1024
+            collective_id=0, has_side_effects=True, vmem_limit_bytes=26 * 1024 * 1024
         ),
     )(*args)
+    results = pl.pallas_call(
+        flush,
+        name="flush",
+        out_shape=[jax.ShapeDtypeStruct(x.shape, x.dtype) for x in args[:9]],
+        in_specs=[pl.BlockSpec(memory_space=pl.ANY)] * 9,
+        out_specs=[pl.BlockSpec(memory_space=pl.ANY)] * 9,
+        scratch_shapes=[dma((9,))],
+        compiler_params=pltpu.CompilerParams(vmem_limit_bytes=1024 * 1024),
+    )(*results)
     return (
         results[0], results[1], results[2], results[3],
         results[4].reshape(owner_weights.shape), results[5].reshape(owner_momentum.shape),
-        results[6], results[7][None, None], results[8][None, None],
+        results[6],
+        jnp.transpose(results[7].reshape(ROWS, 1, WIDTH), (1, 0, 2))[None],
+        results[8].T[None, None],
     )
 
 

time: 70.3 us -> 56.1 us (0.80)
  local copies, waits for them, and re-layouts: 14.9 us -> 0 us
  Pallas kernels: 54.4 us -> 55.3 us
    unnamed x34 -> x0, local copies, waits for them, and re-layouts: 14.9 us -> none
    pallas_call x0 -> x1, Pallas kernels: none -> 2.55 us  [local(): pl.pallas_call(flush, name='flush', out_shape=[jax.ShapeDtypeStruct(x.sha...]
    pallas_call x1, Pallas kernels: 54.4 us -> 52.8 us  [local(): pl.pallas_call(kernel, name='outer_step', out_shape=[jax.ShapeDtypeStruct...]
where the time goes in v1:
time: 56.1 us; the launch traced here: 56 us
  Pallas kernels  55.3 us (99%)
  between operations  0.65 us (1%)
    pallas_call x1, Pallas kernels, local(): pl.pallas_call(kernel, name='outer_step', out_shape=[jax.ShapeDtypeStruct...  52.8 us
    pallas_call x1, Pallas kernels, local(): pl.pallas_call(flush, name='flush', out_shape=[jax.ShapeDtypeStruct(x.sha...  2.55 us

profile of v1, /device:TPU:0, one launch (start us, length us, event | category | flops | bytes accessed | tf_op | source)
XLA Modules:
  0.0 56.0 jit_solution(17815726553119686499)
XLA Ops:
  0.6 52.8 %outer_step.1 = (bf16[2,48,1152]{2,1,0:T(8,128)(2,1)S(1)}, bf16[2,48,384]{2,1,0:T(8,128)(2,1)S(1)}, bf16[2,48,1536]{2,1,0:T(8,128)(2,1)S(1)}, bf16[2,192,384]{2,...) custom-call(bf16[2,48,1152]{2,1,0:T(8,128)(2,1)} %bitcast.25, ...), custom_call_target="tpu_custom_call" | custom-call | tf_op jit(solution)/shard_map/outer_step/pallas_call | solution.py:427
  53.5 2.5 %flush.1 = (bf16[2,48,1152]{2,1,0:T(8,128)(2,1)}, bf16[2,48,384]{2,1,0:T(8,128)(2,1)}, bf16[2,48,1536]{2,1,0:T(8,128)(2,1)}, bf16[2,192,384]{2,1,0:T(8,128)(2,1)...) custom-call(bf16[2,48,1152]{2,1,0:T(8,128)(2,1)S(1)} %get-tuple-elem, ...), custom_call_target="tpu_custom_call" | custom-call | tf_op jit(solution)/shard_map/flush/pallas_call | solution.py:469

commit v2 on v1

--- a/solution.py
+++ b/solution.py
@@ -232,7 +232,7 @@
            z_copy(cf_send.at[left, 0], cf_recv.at[3], left)]
     rs2 = [z_copy(rs_send.at[right, 1], rs_recv.at[1], right),
            z_copy(rs_send.at[left, 0], rs_recv.at[3], left)]
-    for c in cf1 + cf2 + rs2:
+    for c in cf1 + cf2:
         c.start()
 
     for c in cf1:
@@ -241,7 +241,7 @@
     cf_merge[1] = (cf_send[left, 1].astype(F32) + cf_mid[1].astype(F32)).astype(BF16)
     cf3 = [z_copy(cf_merge.at[0], cf_recv.at[0], right),
            z_copy(cf_merge.at[1], cf_recv.at[2], left)]
-    for c in cf3:
+    for c in cf3 + rs2:
         c.start()
 
     for c in rs1:
@@ -253,22 +253,56 @@
     for c in rs3:
         c.start()
 
-    for c in cf2 + cf3:
-        c.wait_recv()
-
-    def total(send, recv):
-        top = send[r, 0].astype(F32) + (recv[0].astype(F32) + recv[3].astype(F32))
-        low = send[r, 1].astype(F32) + (recv[1].astype(F32) + recv[2].astype(F32))
-        return top, low
-
-    top, low = total(cf_send, cf_recv)
-    tp_send[pl.ds(0, HALF), :] = top.astype(BF16)
-    tp_send[pl.ds(HALF, HALF), :] = low.astype(BF16)
-    tp = pltpu.make_async_remote_copy(
-        src_ref=tp_send, dst_ref=tp_recv, send_sem=tp_ss.at[0], recv_sem=tp_rs.at[0],
-        device_id={"tp": 1 - t}, device_id_type=MESH,
-    )
-    tp.start()
+    def total(send, recv, half):
+        near, far = (recv[0], recv[3]) if half == 0 else (recv[1], recv[2])
+        return send[r, half].astype(F32) + (near.astype(F32) + far.astype(F32))
+
+    tp = []
+    for half, arrived in enumerate(([cf2[1], cf3[0]], [cf2[0], cf3[1]])):
+        for c in arrived:
+            c.wait_recv()
+        tp_send[half] = total(cf_send, cf_recv, half).astype(BF16)
+        tp.append(pltpu.make_async_remote_copy(
+            src_ref=tp_send.at[half], dst_ref=tp_recv.at[half],
+            send_sem=tp_ss.at[half], recv_sem=tp_rs.at[half],
+            device_id={"tp": 1 - t}, device_id_type=MESH,
+        ))
+        tp[half].start()
+
+    for c in ins[6:8]:
+        c.wait()
+    momenta = jnp.transpose(em[...])
+    halves = (pl.ds(0, 2 * HALF), pl.ds(2 * HALF, STAGE - 2 * HALF))
+    kept, eg1, eg2 = {}, [], []
+    for half, pieces in enumerate(
+        (((0, 0, HALF), (2 * HALF, HALF, HALF)),
+         ((HALF, 2 * HALF, HALF), (3 * HALF, 3 * HALF, ROWS - 3 * HALF)))
+    ):
+        tp[half].wait_recv()
+        both = (tp_send[half].astype(F32) + tp_recv[half].astype(F32)) * 0.25
+        for (start, at, rows), c in zip(pieces, (both, turn(both, RANK))):
+            c = c[:rows, :RANK]
+            momentum = MOMENTUM * momenta[start : start + rows] + c
+            kept[start] = momentum
+            direction = c + MOMENTUM * momentum
+            d_hi = direction.astype(BF16)
+            d_lo = (direction - d_hi.astype(F32)).astype(BF16)
+            update = jnp.dot(d_hi, b_hi, preferred_element_type=F32)
+            update += jnp.dot(d_lo, b_hi, preferred_element_type=F32)
+            update += jnp.dot(d_hi, b_lo, preferred_element_type=F32)
+            parts = []
+            for j in range(WIDTH // 128):
+                place_of = pl.ds(3 * start + j, rows, 3)
+                table = eo[place_of, :] - OUTER_RATE * tile(update, j)
+                ne[place_of, :] = table
+                parts.append(table.astype(BF16))
+            stage[r, pl.ds(at, rows), :] = jnp.concatenate(parts, axis=1)
+        block = halves[half]
+        far, near = (right, left) if half == 0 else (left, right)
+        eg1.append(z_copy(stage.at[r, block], stage.at[r, block], far))
+        eg2.append(z_copy(stage.at[r, block], stage.at[r, block], near))
+        eg1[half].start()
+        eg2[half].start()
 
     def exchange(send, recv, send_sem, recv_sem):
         copies = [
@@ -286,41 +320,11 @@
 
     for c in rs2 + rs3:
         c.wait_recv()
-    top, low = total(rs_send, rs_recv)
+    top, low = total(rs_send, rs_recv, 0), total(rs_send, rs_recv, 1)
     split_columns(kinds_of(top * 0.25, low * 0.25), a1_send)
     a1 = exchange(a1_send, a1_recv, a1_ss, a1_rs)
 
-    for c in ins[6:8]:
-        c.wait()
-    tp.wait_recv()
-    both = (tp_send[...].astype(F32) + tp_recv[...].astype(F32)) * 0.25
-    momenta = jnp.transpose(em[...])
-    kept = []
-    for start, rows, c in ((0, PACK, both), (PACK, ROWS - PACK, turn(both, RANK))):
-        c = c[:rows, :RANK]
-        momentum = MOMENTUM * momenta[start : start + rows] + c
-        kept.append(momentum)
-        direction = c + MOMENTUM * momentum
-        d_hi = direction.astype(BF16)
-        d_lo = (direction - d_hi.astype(F32)).astype(BF16)
-        update = jnp.dot(d_hi, b_hi, preferred_element_type=F32)
-        update += jnp.dot(d_lo, b_hi, preferred_element_type=F32)
-        update += jnp.dot(d_hi, b_lo, preferred_element_type=F32)
-        parts = []
-        for j in range(WIDTH // 128):
-            place_of = pl.ds(3 * start + j, rows, 3)
-            table = eo[place_of, :] - OUTER_RATE * tile(update, j)
-            ne[place_of, :] = table
-            parts.append(table.astype(BF16))
-        stage[r, pl.ds(start, rows), :] = jnp.concatenate(parts, axis=1)
-    first, second = pl.ds(0, STAGE // 2), pl.ds(STAGE // 2, STAGE // 2)
-    eg1 = [z_copy(stage.at[r, first], stage.at[r, first], right),
-           z_copy(stage.at[r, second], stage.at[r, second], left)]
-    eg2 = [z_copy(stage.at[r, second], stage.at[r, second], right),
-           z_copy(stage.at[r, first], stage.at[r, first], left)]
-    for c in eg1 + eg2:
-        c.start()
-    nem[...] = jnp.transpose(jnp.concatenate(kept, axis=0))
+    nem[...] = jnp.transpose(jnp.concatenate([kept[k] for k in sorted(kept)], axis=0))
     outs = [pltpu.make_async_copy(a, o, out_sem.at[i])
             for i, (a, o) in enumerate([(nem, nem_h), (ne, ne_h), (mn, mn_h), (wn, wn_h),
                                         (fin, fin_h), (fmix, fmix_h), (fexp, fexp_h),
@@ -341,6 +345,12 @@
     a2 = exchange(a2_send, a2_recv, a2_ss, a2_rs)
     for c in outs[2:4]:
         c.start()
+    for c in eg1:
+        c.wait_recv()
+    eg3 = [z_copy(stage.at[left, halves[0]], stage.at[left, halves[0]], right),
+           z_copy(stage.at[right, halves[1]], stage.at[right, halves[1]], left)]
+    for c in eg3:
+        c.start()
 
     for c in a2:
         c.wait_recv()
@@ -354,12 +364,6 @@
     for c in dg1 + dg2:
         c.start()
 
-    for c in eg1:
-        c.wait_recv()
-    eg3 = [z_copy(stage.at[left, first], stage.at[left, first], right),
-           z_copy(stage.at[right, second], stage.at[right, second], left)]
-    for c in eg3:
-        c.start()
     for c in dg1:
         c.wait_recv()
     dg3 = [z_copy(ag.at[left, 0], ag.at[left, 0], right),
@@ -367,10 +371,21 @@
     for c in dg3:
         c.start()
 
-    for c in eg2 + eg3:
+    def assemble(q):
+        for to, at, rows in (
+            (0, 0, HALF), (HALF, 2 * HALF, HALF), (2 * HALF, HALF, HALF),
+            (3 * HALF, 3 * HALF, ROWS - 3 * HALF),
+        ):
+            fe[pl.ds(ROWS * q + to, rows), :] = stage[q, pl.ds(at, rows), :]
+
+    for c in eg2:
         c.wait_recv()
     for q in range(GROUPS):
-        fe[pl.ds(ROWS * q, ROWS), :] = stage[q, pl.ds(0, ROWS), :]
+        pl.when(q != opp)(lambda q=q: assemble(q))
+    for c in eg3:
+        c.wait_recv()
+    for q in range(GROUPS):
+        pl.when(q == opp)(lambda q=q: assemble(q))
     outs[8].start()
 
     for c in dg2 + dg3:
@@ -388,7 +403,7 @@
     for c in outs[4:8]:
         c.start()
 
-    for c in (rs1 + rs2 + rs3 + cf1 + cf2 + cf3 + [tp] + a1 + a2 + eg1 + eg2 + eg3
+    for c in (rs1 + rs2 + rs3 + cf1 + cf2 + cf3 + tp + a1 + a2 + eg1 + eg2 + eg3
               + dg1 + dg2 + dg3):
         c.wait_send()
     for c in outs:
@@ -448,8 +463,8 @@
             pltpu.VMEM((2, HALF, 128), BF16),
             pltpu.VMEM((2, HALF, 128), BF16),
             pltpu.VMEM((4, HALF, 128), BF16),
-            pltpu.VMEM((PACK, 128), BF16),
-            pltpu.VMEM((PACK, 128), BF16),
+            pltpu.VMEM((2, HALF, 128), BF16),
+            pltpu.VMEM((2, HALF, 128), BF16),
             pltpu.VMEM((GROUPS, STAGE, WIDTH), BF16),
             dma((10,)),
             dma((9,)),
@@ -459,8 +474,8 @@
             dma((PEERS,)),
             dma((PEERS,)),
             dma((PEERS,)),
-            dma((1,)),
-            dma((1,)),
+            dma((2,)),
+            dma((2,)),
         ],
         compiler_params=pltpu.CompilerParams(
             collective_id=0, has_side_effects=True, vmem_limit_bytes=26 * 1024 * 1024

time: 56.1 us -> 55.8 us (level)
  no operation moved by 1% of the time
where the time goes in v2:
time: 55.8 us; the launch traced here: 55.7 us
  Pallas kernels  55 us (99%)
  between operations  0.65 us (1%)
    pallas_call x1, Pallas kernels, local(): pl.pallas_call(kernel, name='outer_step', out_shape=[jax.ShapeDtypeStruct...  52.5 us
    pallas_call x1, Pallas kernels, local(): pl.pallas_call(flush, name='flush', out_shape=[jax.ShapeDtypeStruct(x.sha...  2.55 us

profile of v2, /device:TPU:0, one launch (start us, length us, event | category | flops | bytes accessed | tf_op | source)
XLA Modules:
  0.0 55.7 jit_solution(8458467365377249513)
XLA Ops:
  0.6 52.5 %outer_step.1 = (bf16[2,48,1152]{2,1,0:T(8,128)(2,1)S(1)}, bf16[2,48,384]{2,1,0:T(8,128)(2,1)S(1)}, bf16[2,48,1536]{2,1,0:T(8,128)(2,1)S(1)}, bf16[2,192,384]{2,...) custom-call(bf16[2,48,1152]{2,1,0:T(8,128)(2,1)} %bitcast.25, ...), custom_call_target="tpu_custom_call" | custom-call | tf_op jit(solution)/shard_map/outer_step/pallas_call | solution.py:442
  53.1 2.5 %flush.1 = (bf16[2,48,1152]{2,1,0:T(8,128)(2,1)}, bf16[2,48,384]{2,1,0:T(8,128)(2,1)}, bf16[2,48,1536]{2,1,0:T(8,128)(2,1)}, bf16[2,192,384]{2,1,0:T(8,128)(2,1)...) custom-call(bf16[2,48,1152]{2,1,0:T(8,128)(2,1)S(1)} %get-tuple-elem, ...), custom_call_target="tpu_custom_call" | custom-call | tf_op jit(solution)/shard_map/flush/pallas_call | solution.py:484

commit v3 on v2

--- a/solution.py
+++ b/solution.py
@@ -21,7 +21,8 @@
 PACK = 416
 HALF = 208
 STAGE = 800
-CHUNK = 448
+SPAN = 808
+OVER = 48
 
 W_IN, W_MIX, W_EXP, W_RED = 72, 24, 96, 24
 
@@ -149,8 +150,8 @@
     ins = [
         pltpu.make_async_copy(a, b, in_sem.at[i])
         for i, (a, b) in enumerate(
-            [(din_h, din), (dmix_h, dmix), (dexp_h, dexp), (dred_h, dred), (basis_h, basis),
-             (de_h, de), (em_h, em), (eo_h.at[:, 0, :], eo), (w_h, w), (m_h, m)]
+            [(basis_h, basis), (de_h, de), (din_h, din), (dmix_h, dmix), (dexp_h, dexp),
+             (dred_h, dred), (em_h, em), (eo_h.at[:, 0, :], eo), (w_h, w), (m_h, m)]
         )
     ]
     for c in ins:
@@ -175,7 +176,45 @@
             device_id={"rep": to}, device_id_type=MESH,
         )
 
-    for c in ins[:4]:
+    ins[0].wait()
+    b = basis[...]
+    b_hi = b.astype(BF16)
+    b_lo = (b - b_hi.astype(F32)).astype(BF16)
+    rhs = jnp.concatenate([b_hi, b_hi, b_lo, b_lo], axis=0)
+    across = (((1,), (1,)), ((), ()))
+    lane = lanes(PACK)
+    for k in range(GROUPS):
+        coef[k, pl.ds(SPAN, OVER), :] = jnp.zeros((OVER, 128), F32)
+    ins[1].wait()
+
+    def terms(k, q):
+        start = pl.multiple_of(784 * q - 16 * (q // 3), 16)
+        for at, rows in ((0, 400), (400, SPAN - 400)):
+            y = lax.dot_general(
+                de[pl.ds(start + at, rows), :], rhs, across, preferred_element_type=F32
+            )
+            coef[k, pl.ds(at, rows), :] = y[:, :128] + y[:, 128:]
+        skip = 2 * q + 16 * (q // 3)
+        packed = jnp.where(
+            lane < RANK, coef[k, pl.ds(skip, PACK), :], coef[k, pl.ds(skip + PACK, PACK), :]
+        ).astype(BF16)
+        cf_send[q, 0] = packed[:HALF]
+        cf_send[q, 1] = packed[HALF:]
+
+    terms(0, opp)
+    pl.semaphore_wait(barrier, PEERS + 2)
+    cf1 = [z_copy(cf_send.at[opp, 0], cf_mid.at[0], right),
+           z_copy(cf_send.at[opp, 1], cf_mid.at[1], left)]
+    for c in cf1:
+        c.start()
+    terms(1, right)
+    terms(2, left)
+    cf2 = [z_copy(cf_send.at[right, 1], cf_recv.at[1], right),
+           z_copy(cf_send.at[left, 0], cf_recv.at[3], left)]
+    for c in cf2:
+        c.start()
+
+    for c in ins[2:6]:
         c.wait()
 
     def pack(q, ref):
@@ -192,48 +231,14 @@
         rs_send[q, 0] = top.astype(BF16)
         rs_send[q, 1] = low.astype(BF16)
 
-    pl.semaphore_wait(barrier, PEERS + 2)
     rs1 = [z_copy(rs_send.at[opp, 0], rs_mid.at[0], right),
            z_copy(rs_send.at[opp, 1], rs_mid.at[1], left)]
     for c in rs1:
         c.start()
 
-    ins[4].wait()
-    b = basis[...]
-    b_hi = b.astype(BF16)
-    b_lo = (b - b_hi.astype(F32)).astype(BF16)
-    rhs = jnp.concatenate([b_hi, b_hi, b_lo, b_lo], axis=0)
-    across = (((1,), (1,)), ((), ()))
-    ins[5].wait()
-
-    def terms(start, rows):
-        y = lax.dot_general(
-            de[pl.ds(start, rows), :], rhs, across, preferred_element_type=F32
-        )
-        coef[pl.ds(start, rows), :] = y[:, :128] + y[:, 128:]
-
-    def body(i, carry):
-        terms(pl.multiple_of(i * CHUNK, CHUNK), CHUNK)
-        return carry
-
-    lax.fori_loop(0, VROWS // CHUNK, body, 0)
-    terms(VROWS // CHUNK * CHUNK, VROWS % CHUNK)
-    coef[pl.ds(VROWS, 56), :] = jnp.zeros((56, 128), F32)
-    lane = lanes(PACK)
-    for q in range(GROUPS):
-        packed = jnp.where(
-            lane < RANK, coef[pl.ds(ROWS * q, PACK), :], coef[pl.ds(ROWS * q + PACK, PACK), :]
-        ).astype(BF16)
-        cf_send[q, 0] = packed[:HALF]
-        cf_send[q, 1] = packed[HALF:]
-    cf1 = [z_copy(cf_send.at[opp, 0], cf_mid.at[0], right),
-           z_copy(cf_send.at[opp, 1], cf_mid.at[1], left)]
-    cf2 = [z_copy(cf_send.at[right, 1], cf_recv.at[1], right),
-           z_copy(cf_send.at[left, 0], cf_recv.at[3], left)]
+    terms(3, r)
     rs2 = [z_copy(rs_send.at[right, 1], rs_recv.at[1], right),
            z_copy(rs_send.at[left, 0], rs_recv.at[3], left)]
-    for c in cf1 + cf2:
-        c.start()
 
     for c in cf1:
         c.wait_recv()
@@ -458,7 +463,7 @@
             pltpu.VMEM((PEERS, 24, 384), BF16),
             pltpu.VMEM((FLAT_ROWS, 128), F32),
             pltpu.VMEM((GROUPS, 2) + half, BF16),
-            pltpu.VMEM((VROWS + 56, 128), F32),
+            pltpu.VMEM((GROUPS, SPAN + OVER, 128), F32),
             pltpu.VMEM((GROUPS, 2, HALF, 128), BF16),
             pltpu.VMEM((2, HALF, 128), BF16),
             pltpu.VMEM((2, HALF, 128), BF16),

time: 55.8 us -> 55.8 us (level)
  no operation moved by 1% of the time
where the time goes in v3:
time: 55.8 us; the launch traced here: 55.7 us
  Pallas kernels  55 us (99%)
  between operations  0.65 us (1%)
    pallas_call x1, Pallas kernels, local(): pl.pallas_call(kernel, name='outer_step', out_shape=[jax.ShapeDtypeStruct...  52.5 us
    pallas_call x1, Pallas kernels, local(): pl.pallas_call(flush, name='flush', out_shape=[jax.ShapeDtypeStruct(x.sha...  2.55 us

profile of v3, /device:TPU:0, one launch (start us, length us, event | category | flops | bytes accessed | tf_op | source)
XLA Modules:
  0.0 55.7 jit_solution(6064720378224413230)
XLA Ops:
  0.6 52.5 %outer_step.1 = (bf16[2,48,1152]{2,1,0:T(8,128)(2,1)S(1)}, bf16[2,48,384]{2,1,0:T(8,128)(2,1)S(1)}, bf16[2,48,1536]{2,1,0:T(8,128)(2,1)S(1)}, bf16[2,192,384]{2,...) custom-call(bf16[2,48,1152]{2,1,0:T(8,128)(2,1)} %bitcast.25, ...), custom_call_target="tpu_custom_call" | custom-call | tf_op jit(solution)/shard_map/outer_step/pallas_call | solution.py:447
  53.2 2.5 %flush.1 = (bf16[2,48,1152]{2,1,0:T(8,128)(2,1)}, bf16[2,48,384]{2,1,0:T(8,128)(2,1)}, bf16[2,48,1536]{2,1,0:T(8,128)(2,1)}, bf16[2,192,384]{2,1,0:T(8,128)(2,1)...) custom-call(bf16[2,48,1152]{2,1,0:T(8,128)(2,1)S(1)} %get-tuple-elem, ...), custom_call_target="tpu_custom_call" | custom-call | tf_op jit(solution)/shard_map/flush/pallas_call | solution.py:489

commit v4 on v3

--- a/solution.py
+++ b/solution.py
@@ -18,8 +18,8 @@
 WIDTH = 384
 RANK = 64
 FLAT_ROWS = 864
-PACK = 416
-HALF = 208
+PACK = 400
+HALF = 200
 STAGE = 800
 SPAN = 808
 OVER = 48

time: 55.8 us -> 56 us (level)
  no operation moved by 1% of the time
where the time goes in v4:
time: 56 us; the launch traced here: 55.9 us
  Pallas kernels  55.2 us (99%)
  between operations  0.65 us (1%)
    pallas_call x1, Pallas kernels, local(): pl.pallas_call(kernel, name='outer_step', out_shape=[jax.ShapeDtypeStruct...  52.7 us
    pallas_call x1, Pallas kernels, local(): pl.pallas_call(flush, name='flush', out_shape=[jax.ShapeDtypeStruct(x.sha...  2.55 us

profile of v4, /device:TPU:0, one launch (start us, length us, event | category | flops | bytes accessed | tf_op | source)
XLA Modules:
  0.0 55.9 jit_solution(8451244649490817390)
XLA Ops:
  0.6 52.7 %outer_step.1 = (bf16[2,48,1152]{2,1,0:T(8,128)(2,1)S(1)}, bf16[2,48,384]{2,1,0:T(8,128)(2,1)S(1)}, bf16[2,48,1536]{2,1,0:T(8,128)(2,1)S(1)}, bf16[2,192,384]{2,...) custom-call(bf16[2,48,1152]{2,1,0:T(8,128)(2,1)} %bitcast.25, ...), custom_call_target="tpu_custom_call" | custom-call | tf_op jit(solution)/shard_map/outer_step/pallas_call | solution.py:447
  53.3 2.5 %flush.1 = (bf16[2,48,1152]{2,1,0:T(8,128)(2,1)}, bf16[2,48,384]{2,1,0:T(8,128)(2,1)}, bf16[2,48,1536]{2,1,0:T(8,128)(2,1)}, bf16[2,192,384]{2,1,0:T(8,128)(2,1)...) custom-call(bf16[2,48,1152]{2,1,0:T(8,128)(2,1)S(1)} %get-tuple-elem, ...), custom_call_target="tpu_custom_call" | custom-call | tf_op jit(solution)/shard_map/flush/pallas_call | solution.py:489
